TPU v7x, 128 devices: a whole 4x4x4 slice. The times are simulated.
128 devices in a mesh: grp: 8 (over y, core), nbr: 16 (over x, z).
Axes of the slice: x: 4, y: 4, z: 4, core: 2. Of those that a mesh axis runs over, the one named last changes fastest.
Arguments:
- sims: float32 [2048, 128, 128], P(('grp', 'nbr')), may hold values from -6 to 6
- own_tiles: float32 [24576, 128, 128], P(('grp', 'nbr')), may hold values from -0.15625 to 0.15625
- own_cols: int32 [24576], P(('grp', 'nbr')), may hold values from 0 to 271
- own_rows: int32 [24576], P(('grp', 'nbr')), may hold values from 0 to 15
- help_tiles: float32 [4096, 128, 128], P(('grp', 'nbr')), may hold values from -0.15625 to 0.15625
- help_cols: int32 [4096], P(('grp', 'nbr')), may hold values from 0 to 271
- help_rows: int32 [4096], P(('grp', 'nbr')), may hold values from 0 to 15
- help_live: int32 [4096], P(('grp', 'nbr')), may hold values from 0 to 1, as said below
Outputs:
- reobserved: float32 [2048, 128, 128], P(('grp', 'nbr'))
Inputs may be any that keep to these rules, and one draw needn't show every extreme that they name: `help_live`: helper slot j of a device serves the owner of neighbour index j // 2 in the same group, so at most 2 live slots go from one device to one owner; in every group one owner receives all 2 slots live from every device of the group.
All inputs are finite; a program needn't handle non-finite values.
Results may differ from a plain program's by a relative error of at most 0.0001.
Values sent between devices are 32-bit elements; how exact they have to be, the bound alone decides.
A program may use at most 192 MiB of HBM per device.

v0:
```python
import jax
import jax.numpy as jnp
from jax import lax
from jax.sharding import PartitionSpec as P

RIM = 8


def padded(shard, sides, width):
    for axis, dim in sides:
        peers, length = (lax.axis_size(axis), shard.shape[dim])
        up = [(i, (i + 1) % peers) for i in range(peers - 1)]
        down = [(j, i) for i, j in up]
        last = lax.slice_in_dim(shard, length - width, length, axis=dim)
        initial = lax.slice_in_dim(shard, 0, width, axis=dim)
        before = lax.ppermute(last, axis, up)
        after = lax.ppermute(initial, axis, down)
        shard = jnp.concatenate([before, shard, after], axis=dim)
    return shard


def pick_from(source, first, cols):
    length = source.shape[0]
    index = cols - first
    valid = ((index >= 0) & (index < length)).astype(jnp.float32)
    taken = jnp.take(source, jnp.clip(index, 0, length - 1), axis=0)
    return taken * valid[:, None, None]


def local(sims, own_tiles, own_cols, own_rows, help_tiles, help_cols, help_rows, help_live):
    high = lax.Precision.HIGHEST
    rows_dev = sims.shape[0]
    neighbours = lax.axis_size("nbr")
    group_rows = rows_dev * neighbours
    help_dev = help_tiles.shape[0]
    slots_owner = help_dev // neighbours
    group = lax.all_gather(sims, "nbr", axis=0, tiled=True)
    own_pick = pick_from(group, RIM, own_cols)
    help_pick = pick_from(group, RIM, help_cols)
    edges = jnp.concatenate([group[:RIM], group[group_rows - RIM :]], axis=0)
    rims = padded(edges, (("grp", 0),), RIM)
    lower = rims[:RIM]
    upper = rims[rims.shape[0] - RIM :]
    own_pick = (
        own_pick + pick_from(lower, 0, own_cols) + pick_from(upper, RIM + group_rows, own_cols)
    )
    help_pick = (
        help_pick + pick_from(lower, 0, help_cols) + pick_from(upper, RIM + group_rows, help_cols)
    )
    own_terms = jnp.einsum("tij,tjs->tis", own_tiles, own_pick, precision=high)
    select = (own_rows[None, :] == jnp.arange(rows_dev, dtype=jnp.int32)[:, None]).astype(
        jnp.float32
    )
    own_sum = jnp.einsum("rt,tis->ris", select, own_terms, precision=high)
    help_terms = (
        jnp.einsum("tij,tjs->tis", help_tiles, help_pick, precision=high)
        * help_live.astype(jnp.float32)[:, None, None]
    )
    outgoing = help_terms.reshape(neighbours, slots_owner, help_terms.shape[1], help_terms.shape[2])
    out_rows = help_rows.astype(jnp.float32).reshape(neighbours, slots_owner)
    incoming, in_rows = (
        lax.all_to_all(outgoing, "nbr", split_axis=0, concat_axis=0, tiled=True),
        lax.all_to_all(out_rows, "nbr", split_axis=0, concat_axis=0, tiled=True),
    )
    flat_terms = incoming.reshape(help_dev, incoming.shape[2], incoming.shape[3])
    flat_rows = in_rows.reshape(help_dev)
    picker = (flat_rows[None, :] == jnp.arange(rows_dev, dtype=jnp.float32)[:, None]).astype(
        jnp.float32
    )
    help_sum = jnp.einsum("rt,tis->ris", picker, flat_terms, precision=high)
    return own_sum + help_sum


def solution(mesh):
    placed = (
        P(("grp", "nbr"), None, None),
        P(("grp", "nbr"), None, None),
        P(("grp", "nbr")),
        P(("grp", "nbr")),
        P(("grp", "nbr"), None, None),
        P(("grp", "nbr")),
        P(("grp", "nbr")),
        P(("grp", "nbr")),
    )
    return jax.shard_map(
        local, mesh=mesh, in_specs=placed, out_specs=P(("grp", "nbr"), None, None), check_vma=False
    )
```

profile of v0, /device:TPU:1, one launch (start us, length us, event | category | flops | bytes accessed | tf_op | source)
XLA Modules:
  0.0 253.4 jit_solution(752253415979622065)
XLA Ops:
  6.5 0.0 copy-start
  6.5 0.0 copy-start.2
  6.5 0.0 copy-start.4
  6.5 0.0 all-gather.2.cloned.1.call-start
  6.5 0.7 all-gather.2.cloned.1.call-update
  7.3 0.7 convert_element_type.29
  7.9 0.7 all_to_all.9
  8.6 8.4 %all-to-all-start = ((f32[16,1,2]{2,1,0:T(1,128)}), f32[16,1,2]{2,1,0:T(1,128)S(1)}, u32[]{:S(2)}, u32[]{:S(2)}) async-start(f32[16,1,2]{2,1,0:T(1,128)} %bitcast.2), calls=%async_computation | async-start | bytes 16384 | tf_op jit(solution)/shard_map/all_to_all | solution.py:63
  17.0 0.7 compare_select_fusion.1
  17.7 0.7 and_convert_fusion.2
  18.4 105.5 %all-gather.2.cloned.1.call-done = f32[256,128,128]{2,1,0:T(8,128)} async-done(((f32[16,128,128]{2,1,0:T(8,128)}), f32[256,128,128]{2,1,0:T(8,128)}) %all-gather.2.cloned.1.call-update) | async-done | bytes 16777232 | tf_op jit(solution)/shard_map/all_gather | solution.py:37
  123.9 2.3 fusion.43
  126.1 3.8 %collective-permute-start = (f32[8,128,128]{2,1,0:T(8,128)}, f32[8,128,128]{2,1,0:T(8,128)S(1)}, u32[]{:S(2)}, u32[]{:S(2)}) collective-permute-start(f32[8,128,128]{2,1,0:T(8,128)} %get-tuple-element.17), channel_id=1, source_target_pairs={{0,16},{16,32},{32,48},{48,64},{64,80},{80,96},{96,112},{1,17},{17... | collective-permute-start | bytes 1572872 | tf_op jit(solution)/shard_map/ppermute | solution.py:16
  130.0 1.9 collective-permute-start.1
  131.9 0.0 copy-done.2
  132.0 0.0 copy-done.4
  132.0 0.0 all-to-all-done
  132.0 0.5 broadcast.82
  132.5 0.6 reduce.3
  133.1 0.1 eq.31
  133.2 7.7 %gather_fusion.1 = f32[32,128,128]{2,1,0:T(8,128)} fusion(f32[256,128,128]{2,1,0:T(8,128)} %all-gather.2.cloned.1.call-done, s32[1024]{0:T(1024)S(1)} %pad_clamp_fusion.2), kind=kCustom, calls=%fused_computation.5 | custom fusion | bytes 4194432 | tf_op jit(solution)/shard_map/jit(_take)/gather | solution.py:26
  140.9 16.5 %gather_fusion = f32[192,128,128]{2,1,0:T(8,128)} fusion(f32[256,128,128]{2,1,0:T(8,128)} %all-gather.2.cloned.1.call-done, s32[1024]{0:T(1024)S(1)} %get-tuple-element.37), kind=kCustom, calls=%fused_computation.4 | custom fusion | bytes 25166592 | tf_op jit(solution)/shard_map/jit(_take)/gather | solution.py:26
  157.4 0.0 collective-permute-done.1
  157.4 2.0 gather_fusion.5
  159.4 0.0 collective-permute-done
  159.4 2.0 gather_fusion.4
  161.4 0.0 copy-done
  161.4 8.3 %fusion.24 = f32[32,128,128]{2,1,0:T(8,128)} fusion(f32[32,128,128]{2,1,0:T(8,128)S(1)} %copy-done, f32[32,128,128]{2,1,0:T(8,128)} %gather_fusion.5, f32[32,128,128]{2,1,0:T(8,128)} %gather_fusion.4, f32[32,128,128]{2,1,0:T(8,128)} %gather_fusion.1, f32[32]{0:T(128)S(1)} %convert_element_type.33, f32[32]{0:T(128)S(1)} %get-tuple-element.28, ...), kind=kOutput, calls=%fused_computation.28 | convolution fusion | flops 810024960 | bytes 10486368 | tf_op jit(solution)/shard_map/tij,tjs->tis/dot_general | solution.py:56
  169.8 5.0 %all-to-all-start.1 = ((f32[16,2,128,128]{2,3,1,0:T(8,128)}), f32[16,2,128,128]{2,3,1,0:T(8,128)S(1)}, u32[]{:S(2)}, u32[]{:S(2)}) async-start(f32[16,2,128,128]{2,3,1,0:T(8,128)} %bitcast.18), calls=%async_computation.1 | async-start | bytes 4194304 | tf_op jit(solution)/shard_map/all_to_all | solution.py:62
  174.8 5.9 %gather_fusion.2 = f32[192,128,128]{2,1,0:T(8,128)} fusion(f32[8,128,128]{2,1,0:T(8,128)S(1)} %collective-permute-done, s32[1024]{0:T(1024)S(1)} %pad_clamp_fusion.4), kind=kCustom, calls=%fused_computation.clone | custom fusion | bytes 25166592 | tf_op jit(solution)/shard_map/jit(_take)/gather | solution.py:26
  180.7 5.9 %gather_fusion.3 = f32[192,128,128]{2,1,0:T(8,128)} fusion(f32[8,128,128]{2,1,0:T(8,128)S(1)} %collective-permute-done.1, s32[1024]{0:T(1024)S(1)} %get-tuple-element.36), kind=kCustom, calls=%fused_computation.2.clone | custom fusion | bytes 25166592 | tf_op jit(solution)/shard_map/jit(_take)/gather | solution.py:26
  186.6 33.9 %fusion.14 = f32[192,128,128]{1,2,0:T(8,128)} fusion(f32[192,128,128]{2,1,0:T(8,128)} %param.13, f32[192,128,128]{2,1,0:T(8,128)} %gather_fusion.3, f32[192,128,128]{2,1,0:T(8,128)} %gather_fusion.2, f32[192,128,128]{2,1,0:T(8,128)} %gather_fusion, f32[192]{0:T(256)S(1)} %get-tuple-element.21, f32[192]{0:T(256)S(1)} %get-tuple-element.26, ...), kind=kOutput, calls=%fused_computation.20 | convolution fusion | flops 4857004032 | bytes 62917440 | tf_op jit(solution)/shard_map/tij,tjs->tis/dot_general | solution.py:50
  220.4 0.0 copy-start.3
  220.4 12.7 %copy.16 = f32[192,128,128]{2,0,1:T(8,128)} copy(f32[192,128,128]{1,2,0:T(8,128)} %fusion.14) | data formatting | bytes 25165824 | tf_op jit(solution)/shard_map/tij,tjs->tis/dot_general | solution.py:50
  233.2 0.0 copy-done.3
  233.2 7.1 %fusion.35 = f32[16,128,128]{2,0,1:T(8,128)S(1)} fusion(f32[192,128,128]{2,0,1:T(8,128)} %copy.16, s32[192]{0:T(256)S(1)} %copy-done.3), kind=kOutput, calls=%fused_computation.39 | convolution fusion | flops 603982848 | bytes 13632256 | tf_op jit(solution)/shard_map/rt,tis->ris/dot_general | solution.py:54
  240.2 0.0 all-to-all-done.1
  240.2 2.5 copy.19
  242.7 0.0 copy-start.1
  242.7 2.5 %convolution_add_fusion = f32[16,128,128]{2,0,1:T(8,128)S(1)} fusion(f32[16,128,128]{2,0,1:T(8,128)S(1)} %fusion.35, f32[32,128,128]{2,0,1:T(8,128)} %bitcast.17, f32[32]{0:T(128)S(1)} %eq.31), kind=kOutput, calls=%fused_computation.29 | convolution fusion | flops 100925952 | bytes 4194432 | tf_op jit(solution)/shard_map/rt,tis->ris/dot_general | solution.py:70
  245.2 1.3 copy.20
  246.5 0.0 copy-done.1
  (6 shorter events, 0.0 us)
Async XLA Ops:
  6.5 154.9 %copy-start = (f32[32,128,128]{2,1,0:T(8,128)S(1)}, f32[32,128,128]{2,1,0:T(8,128)}, u32[]{:S(2)}) copy-start(f32[32,128,128]{2,1,0:T(8,128)} %param.16) | copy-start | bytes 6291460
  6.5 125.4 %copy-start.2 = (s32[192]{0:T(256)S(1)}, s32[192]{0:T(256)}, u32[]{:S(2)}) copy-start(s32[192]{0:T(256)} %param.14) | copy-start | bytes 2308
  6.5 125.4 %copy-start.4 = (s32[32]{0:T(128)S(1)}, s32[32]{0:T(128)}, u32[]{:S(2)}) copy-start(s32[32]{0:T(128)} %param.19) | copy-start | bytes 388
  6.5 117.3 %all-gather.2.cloned.1.call-start = ((), (), s32[]{:S(2)}) async-start(), calls=%async_computation.2 | async-start | bytes 17825792 | tf_op jit(solution)/shard_map/all_gather | solution.py:37
  8.6 123.4 %all-to-all-start = ((f32[16,1,2]{2,1,0:T(1,128)}), f32[16,1,2]{2,1,0:T(1,128)S(1)}, u32[]{:S(2)}, u32[]{:S(2)}) async-start(f32[16,1,2]{2,1,0:T(1,128)} %bitcast.2), calls=%async_computation | async-start | bytes 16384 | tf_op jit(solution)/shard_map/all_to_all | solution.py:63
  126.1 33.3 %collective-permute-start = (f32[8,128,128]{2,1,0:T(8,128)}, f32[8,128,128]{2,1,0:T(8,128)S(1)}, u32[]{:S(2)}, u32[]{:S(2)}) collective-permute-start(f32[8,128,128]{2,1,0:T(8,128)} %get-tuple-element.17), channel_id=1, source_target_pairs={{0,16},{16,32},{32,48},{48,64},{64,80},{80,96},{96,112},{1,17},{17... | collective-permute-start | bytes 1572872 | tf_op jit(solution)/shard_map/ppermute | solution.py:16
  130.0 27.5 %collective-permute-start.1 = (f32[8,128,128]{2,1,0:T(8,128)}, f32[8,128,128]{2,1,0:T(8,128)S(1)}, u32[]{:S(2)}, u32[]{:S(2)}) collective-permute-start(f32[8,128,128]{2,1,0:T(8,128)} %get-tuple-element.18), channel_id=1, source_target_pairs={{16,0},{32,16},{48,32},{64,48},{80,64},{96,80},{112,96},{17,1},{33... | collective-permute-start | bytes 1572872 | tf_op jit(solution)/shard_map/ppermute | solution.py:17
  169.8 70.5 %all-to-all-start.1 = ((f32[16,2,128,128]{2,3,1,0:T(8,128)}), f32[16,2,128,128]{2,3,1,0:T(8,128)S(1)}, u32[]{:S(2)}, u32[]{:S(2)}) async-start(f32[16,2,128,128]{2,3,1,0:T(8,128)} %bitcast.18), calls=%async_computation.1 | async-start | bytes 4194304 | tf_op jit(solution)/shard_map/all_to_all | solution.py:62
  220.4 12.7 %copy-start.3 = (s32[192]{0:T(256)S(1)}, s32[192]{0:T(256)}, u32[]{:S(2)}) copy-start(s32[192]{0:T(256)} %param.15) | copy-start | bytes 2308
  242.7 3.8 %copy-start.1 = (f32[32,128,128]{2,1,0:T(8,128)S(1)}, f32[32,128,128]{2,1,0:T(8,128)}, u32[]{:S(2)}) copy-start(f32[32,128,128]{2,1,0:T(8,128)} %param.16) | copy-start | bytes 6291460
Sparse Core Ops, SparseCore 0:
  9.5 114.3 all-gather.1
where the time goes:
time: 254 us; the launch traced here: 253 us
  waiting for transfers between devices  106 us (42%)
  local copies, waits for them, and re-layouts  60.1 us (24%)
  matrix products  51.8 us (20%)
  starting transfers between devices  19.2 us (8%)
  between operations  13.5 us (5%)
  other arithmetic  2.63 us (1%)
    all_gather x1, waiting for transfers between devices, local(): group = lax.all_gather(sims, 'nbr', axis=0, tiled=True)  105 us
    gather x6, local copies, waits for them, and re-layouts, pick_from(): taken = jnp.take(source, jnp.clip(index, 0, length - 1), axis=0)  40.1 us
    dot_general x1, matrix products, local(): own_terms = jnp.einsum('tij,tjs->tis', own_tiles, own_pick, precision=high)  33.9 us
    dot_general x1, local copies, waits for them, and re-layouts, local(): own_terms = jnp.einsum('tij,tjs->tis', own_tiles, own_pick, precision=high)  12.7 us
    all_to_all x1, starting transfers between devices, local(): lax.all_to_all(out_rows, 'nbr', split_axis=0, concat_axis=0, tiled=True)  8.42 us
    dot_general x1, matrix products, local(): jnp.einsum('tij,tjs->tis', help_tiles, help_pick, precision=high)  8.31 us
    dot_general x1, matrix products, local(): own_sum = jnp.einsum('rt,tis->ris', select, own_terms, precision=high)  7.07 us
  transfers between devices with their start and end apart: 5, of which 1 were waited for; matrix products, arithmetic and copies ran while one was open for 38% of the time, Pallas kernels for 0%

commit v1 on v0

--- a/solution.py
+++ b/solution.py
@@ -34,7 +34,9 @@
     group_rows = rows_dev * neighbours
     help_dev = help_tiles.shape[0]
     slots_owner = help_dev // neighbours
-    group = lax.all_gather(sims, "nbr", axis=0, tiled=True)
+    group = jnp.concatenate(
+        lax.all_to_all(jnp.stack([sims] * lax.axis_size("nbr")), "nbr", 0, 0), axis=0
+    )
     own_pick = pick_from(group, RIM, own_cols)
     help_pick = pick_from(group, RIM, help_cols)
     edges = jnp.concatenate([group[:RIM], group[group_rows - RIM :]], axis=0)

time: 254 us -> 448 us (1.76)
  waiting for transfers between devices: 106 us -> 293 us
  starting transfers between devices: 19.2 us -> 32.7 us
  between operations: 13.5 us -> 0.18 us
  local copies, waits for them, and re-layouts: 60.1 us -> 69.6 us
    all_to_all x0 -> x1, waiting for transfers between devices: none -> 293 us  [local(): lax.all_to_all(jnp.stack([sims] * lax.axis_size('nbr')), 'nbr', 0, 0)]
    all_gather x1 -> x0, waiting for transfers between devices: 105 us -> none  [local(): group = lax.all_gather(sims, 'nbr', axis=0, tiled=True)]
    another operation x0 -> x1, local copies, waits for them, and re-layouts: none -> 9.35 us  [local(): jnp.stack([sims] * lax.axis_size('nbr'))]
    all_to_all x0 -> x1, starting transfers between devices: none -> 8.61 us  [local(): lax.all_to_all(jnp.stack([sims] * lax.axis_size('nbr')), 'nbr', 0, 0)]
  transfers between devices with their start and end apart: 5 -> 5, of which waited for: 1 -> 1; matrix products, arithmetic and copies ran while one was open for 38% -> 21% of each run, Pallas kernels for 0% -> 0%
where the time goes in v1:
time: 448 us
  waiting for transfers between devices  293 us (65%)
  local copies, waits for them, and re-layouts  69.6 us (16%)
  matrix products  51.8 us (12%)
  starting transfers between devices  32.7 us (7%)
    all_to_all x1, waiting for transfers between devices, local(): lax.all_to_all(jnp.stack([sims] * lax.axis_size('nbr')), 'nbr', 0, 0)  293 us
    gather x6, local copies, waits for them, and re-layouts, pick_from(): taken = jnp.take(source, jnp.clip(index, 0, length - 1), axis=0)  40.1 us
    dot_general x1, matrix products, local(): own_terms = jnp.einsum('tij,tjs->tis', own_tiles, own_pick, precision=high)  33.9 us
    dot_general x1, local copies, waits for them, and re-layouts, local(): own_terms = jnp.einsum('tij,tjs->tis', own_tiles, own_pick, precision=high)  12.8 us
    all_to_all x1, starting transfers between devices, local(): lax.all_to_all(out_rows, 'nbr', split_axis=0, concat_axis=0, tiled=True)  9.95 us
    another operation x1, local copies, waits for them, and re-layouts, local(): jnp.stack([sims] * lax.axis_size('nbr'))  9.35 us
  transfers between devices with their start and end apart: 5, of which 1 were waited for; matrix products, arithmetic and copies ran while one was open for 21% of the time, Pallas kernels for 0%

profile of v1, /device:TPU:1, one launch (start us, length us, event | category | flops | bytes accessed | tf_op | source)
XLA Modules:
  0.0 447.6 jit_solution(10361106851248171014)
XLA Ops:
  0.0 0.0 copy-start
  0.0 9.4 %stack.2 = f32[16,16,128,128]{3,2,1,0:T(8,128)} broadcast(f32[16,128,128]{2,1,0:T(8,128)} %param.12), dimensions={1,2,3} | broadcast | bytes 17825792 | tf_op jit(solution)/shard_map/stack | solution.py:38
  9.4 0.0 copy-start.5
  9.4 0.0 copy-start.2
  9.4 0.0 copy-start.4
  9.4 0.0 copy-start.6
  9.4 8.6 %all-to-all-start = ((f32[16,16,128,128]{3,2,1,0:T(8,128)}), f32[16,16,128,128]{3,2,1,0:T(8,128)}, u32[]{:S(2)}, u32[]{:S(2)}) async-start(f32[16,16,128,128]{3,2,1,0:T(8,128)} %stack.2), calls=%async_computation | async-start | bytes 33554432 | tf_op jit(solution)/shard_map/all_to_all | solution.py:38
  18.0 0.0 copy-done.5
  18.0 0.7 all_to_all.13
  18.7 0.0 copy-done.2
  18.7 0.0 copy-done.4
  18.7 292.6 %all-to-all-done = f32[16,16,128,128]{3,2,1,0:T(8,128)} async-done(((f32[16,16,128,128]{3,2,1,0:T(8,128)}), f32[16,16,128,128]{3,2,1,0:T(8,128)}, u32[]{:S(2)}, u32[]{:S(2)}) %all-to-all-start) | async-done | bytes 16777248 | tf_op jit(solution)/shard_map/all_to_all | solution.py:38
  311.3 9.9 %all-to-all-start.1 = ((f32[16,1,2]{2,1,0:T(1,128)}), f32[16,1,2]{2,1,0:T(1,128)S(1)}, u32[]{:S(2)}, u32[]{:S(2)}) async-start(f32[16,1,2]{2,1,0:T(1,128)} %bitcast.3), calls=%async_computation.1 | async-start | bytes 16384 | tf_op jit(solution)/shard_map/all_to_all | solution.py:65
  321.3 2.3 fusion.43
  323.5 5.3 %collective-permute-start = (f32[8,128,128]{2,1,0:T(8,128)}, f32[8,128,128]{2,1,0:T(8,128)S(1)}, u32[]{:S(2)}, u32[]{:S(2)}) collective-permute-start(f32[8,128,128]{2,1,0:T(8,128)} %get-tuple-element.17), channel_id=1, source_target_pairs={{0,16},{16,32},{32,48},{48,64},{64,80},{80,96},{96,112},{1,17},{17... | collective-permute-start | bytes 1572872 | tf_op jit(solution)/shard_map/ppermute | solution.py:16
  328.8 1.9 collective-permute-start.1
  330.8 0.0 copy-done.6
  330.8 0.0 all-to-all-done.1
  330.8 0.5 broadcast.84
  331.4 0.7 reduce.3
  332.0 0.1 eq.31
  332.1 7.8 %gather_fusion.1 = f32[32,128,128]{2,1,0:T(8,128)} fusion(f32[256,128,128]{2,1,0:T(8,128)} %bitcast.1, s32[1024]{0:T(1024)S(1)} %pad_clamp_fusion.2), kind=kCustom, calls=%fused_computation.5 | custom fusion | bytes 4194432 | tf_op jit(solution)/shard_map/jit(_take)/gather | solution.py:26
  339.9 16.5 %gather_fusion = f32[192,128,128]{2,1,0:T(8,128)} fusion(f32[256,128,128]{2,1,0:T(8,128)} %bitcast.1, s32[1024]{0:T(1024)S(1)} %get-tuple-element.37), kind=kCustom, calls=%fused_computation.4 | custom fusion | bytes 25166592 | tf_op jit(solution)/shard_map/jit(_take)/gather | solution.py:26
  356.4 0.0 collective-permute-done.1
  356.4 2.0 gather_fusion.5
  358.4 0.0 collective-permute-done
  358.4 2.0 gather_fusion.4
  360.4 0.0 copy-done
  360.4 8.3 %fusion.24 = f32[32,128,128]{2,1,0:T(8,128)} fusion(f32[32,128,128]{2,1,0:T(8,128)S(1)} %copy-done, f32[32,128,128]{2,1,0:T(8,128)} %gather_fusion.5, f32[32,128,128]{2,1,0:T(8,128)} %gather_fusion.4, f32[32,128,128]{2,1,0:T(8,128)} %gather_fusion.1, f32[32]{0:T(128)S(1)} %convert_element_type.33, f32[32]{0:T(128)S(1)} %get-tuple-element.28, ...), kind=kOutput, calls=%fused_computation.28 | convolution fusion | flops 810024960 | bytes 10486368 | tf_op jit(solution)/shard_map/tij,tjs->tis/dot_general | solution.py:58
  368.7 6.9 %all-to-all-start.2 = ((f32[16,2,128,128]{2,3,1,0:T(8,128)}), f32[16,2,128,128]{2,3,1,0:T(8,128)S(1)}, u32[]{:S(2)}, u32[]{:S(2)}) async-start(f32[16,2,128,128]{2,3,1,0:T(8,128)} %bitcast.19), calls=%async_computation.2 | async-start | bytes 4194304 | tf_op jit(solution)/shard_map/all_to_all | solution.py:64
  375.7 5.9 %gather_fusion.2 = f32[192,128,128]{2,1,0:T(8,128)} fusion(f32[8,128,128]{2,1,0:T(8,128)S(1)} %collective-permute-done, s32[1024]{0:T(1024)S(1)} %pad_clamp_fusion.4), kind=kCustom, calls=%fused_computation.clone | custom fusion | bytes 25166592 | tf_op jit(solution)/shard_map/jit(_take)/gather | solution.py:26
  381.6 5.9 %gather_fusion.3 = f32[192,128,128]{2,1,0:T(8,128)} fusion(f32[8,128,128]{2,1,0:T(8,128)S(1)} %collective-permute-done.1, s32[1024]{0:T(1024)S(1)} %get-tuple-element.36), kind=kCustom, calls=%fused_computation.2.clone | custom fusion | bytes 25166592 | tf_op jit(solution)/shard_map/jit(_take)/gather | solution.py:26
  387.5 33.9 %fusion.14 = f32[192,128,128]{1,2,0:T(8,128)} fusion(f32[192,128,128]{2,1,0:T(8,128)} %param.13, f32[192,128,128]{2,1,0:T(8,128)} %gather_fusion.3, f32[192,128,128]{2,1,0:T(8,128)} %gather_fusion.2, f32[192,128,128]{2,1,0:T(8,128)} %gather_fusion, f32[192]{0:T(256)S(1)} %get-tuple-element.21, f32[192]{0:T(256)S(1)} %get-tuple-element.26, ...), kind=kOutput, calls=%fused_computation.20 | convolution fusion | flops 4857004032 | bytes 62917440 | tf_op jit(solution)/shard_map/tij,tjs->tis/dot_general | solution.py:52
  421.4 0.0 copy-start.3
  421.4 12.8 %copy.15 = f32[192,128,128]{2,0,1:T(8,128)} copy(f32[192,128,128]{1,2,0:T(8,128)} %fusion.14) | data formatting | bytes 25165824 | tf_op jit(solution)/shard_map/tij,tjs->tis/dot_general | solution.py:52
  434.1 0.0 copy-done.3
  434.1 7.1 %fusion.35 = f32[16,128,128]{2,0,1:T(8,128)S(1)} fusion(f32[192,128,128]{2,0,1:T(8,128)} %copy.15, s32[192]{0:T(256)S(1)} %copy-done.3), kind=kOutput, calls=%fused_computation.39 | convolution fusion | flops 603982848 | bytes 13632256 | tf_op jit(solution)/shard_map/rt,tis->ris/dot_general | solution.py:56
  441.2 0.0 all-to-all-done.2
  441.2 2.5 copy.18
  443.7 0.0 copy-start.1
  443.7 2.5 convolution_add_fusion
  446.3 1.3 copy.19
  447.5 0.0 copy-done.1
  (9 shorter events, 0.1 us)
Async XLA Ops:
  0.0 360.4 %copy-start = (f32[32,128,128]{2,1,0:T(8,128)S(1)}, f32[32,128,128]{2,1,0:T(8,128)}, u32[]{:S(2)}) copy-start(f32[32,128,128]{2,1,0:T(8,128)} %param.16) | copy-start | bytes 6291460
  9.4 8.6 %copy-start.5 = (s32[32]{0:T(128)S(1)}, s32[32]{0:T(128)}, u32[]{:S(2)}) copy-start(s32[32]{0:T(128)} %param.18) | copy-start | bytes 388
  9.4 9.3 %copy-start.2 = (s32[192]{0:T(256)S(1)}, s32[192]{0:T(256)}, u32[]{:S(2)}) copy-start(s32[192]{0:T(256)} %param.14) | copy-start | bytes 2308
  9.4 9.4 %copy-start.4 = (s32[32]{0:T(128)S(1)}, s32[32]{0:T(128)}, u32[]{:S(2)}) copy-start(s32[32]{0:T(128)} %param.17) | copy-start | bytes 388
  9.4 321.4 %copy-start.6 = (s32[32]{0:T(128)S(1)}, s32[32]{0:T(128)}, u32[]{:S(2)}) copy-start(s32[32]{0:T(128)} %param.19) | copy-start | bytes 388
  9.4 301.9 %all-to-all-start = ((f32[16,16,128,128]{3,2,1,0:T(8,128)}), f32[16,16,128,128]{3,2,1,0:T(8,128)}, u32[]{:S(2)}, u32[]{:S(2)}) async-start(f32[16,16,128,128]{3,2,1,0:T(8,128)} %stack.2), calls=%async_computation | async-start | bytes 33554432 | tf_op jit(solution)/shard_map/all_to_all | solution.py:38
  311.3 19.5 %all-to-all-start.1 = ((f32[16,1,2]{2,1,0:T(1,128)}), f32[16,1,2]{2,1,0:T(1,128)S(1)}, u32[]{:S(2)}, u32[]{:S(2)}) async-start(f32[16,1,2]{2,1,0:T(1,128)} %bitcast.3), calls=%async_computation.1 | async-start | bytes 16384 | tf_op jit(solution)/shard_map/all_to_all | solution.py:65
  323.5 34.9 %collective-permute-start = (f32[8,128,128]{2,1,0:T(8,128)}, f32[8,128,128]{2,1,0:T(8,128)S(1)}, u32[]{:S(2)}, u32[]{:S(2)}) collective-permute-start(f32[8,128,128]{2,1,0:T(8,128)} %get-tuple-element.17), channel_id=1, source_target_pairs={{0,16},{16,32},{32,48},{48,64},{64,80},{80,96},{96,112},{1,17},{17... | collective-permute-start | bytes 1572872 | tf_op jit(solution)/shard_map/ppermute | solution.py:16
  328.8 27.6 %collective-permute-start.1 = (f32[8,128,128]{2,1,0:T(8,128)}, f32[8,128,128]{2,1,0:T(8,128)S(1)}, u32[]{:S(2)}, u32[]{:S(2)}) collective-permute-start(f32[8,128,128]{2,1,0:T(8,128)} %get-tuple-element.18), channel_id=1, source_target_pairs={{16,0},{32,16},{48,32},{64,48},{80,64},{96,80},{112,96},{17,1},{33... | collective-permute-start | bytes 1572872 | tf_op jit(solution)/shard_map/ppermute | solution.py:17
  368.7 72.5 %all-to-all-start.2 = ((f32[16,2,128,128]{2,3,1,0:T(8,128)}), f32[16,2,128,128]{2,3,1,0:T(8,128)S(1)}, u32[]{:S(2)}, u32[]{:S(2)}) async-start(f32[16,2,128,128]{2,3,1,0:T(8,128)} %bitcast.19), calls=%async_computation.2 | async-start | bytes 4194304 | tf_op jit(solution)/shard_map/all_to_all | solution.py:64
  421.4 12.8 %copy-start.3 = (s32[192]{0:T(256)S(1)}, s32[192]{0:T(256)}, u32[]{:S(2)}) copy-start(s32[192]{0:T(256)} %param.15) | copy-start | bytes 2308
  443.7 3.8 copy-start.1
